TPU v7x, 32 devices: a whole 2x2x4 slice. The times are simulated.
32 devices in a mesh: gx: 16 (over z, y, core), gy: 2 (over x).
Axes of the slice: x: 2, y: 2, z: 4, core: 2. Of those that a mesh axis runs over, the one named last changes fastest.
Arguments:
- positions: float32 [3, 65536], P(None, ('gx', 'gy')), may hold values from 0 to 6
- features: bfloat16 [64, 65536], P(None, ('gx', 'gy')), may hold values from -6 to 6
- halo_lists: int32 [2, 49152], P(None, ('gx', 'gy')), may hold values from 0 to 2047
- local_pairs: int32 [4, 196608], P(None, ('gx', 'gy')), may hold values from 0 to 2047, as said below
- cross_x: int32 [4, 65536], P(None, ('gx', 'gy')), may hold values from 0 to 2047, as said below
- cross_y: int32 [4, 65536], P(None, ('gx', 'gy')), may hold values from 0 to 2047, as said below
- pair_counts: int32 [32, 3], P(('gx', 'gy')), may hold values from 256 to 6144, as said below
- w_rbf: bfloat16 [8, 256], replicated, may hold values from -2 to 2
- w_src: bfloat16 [64, 256], replicated, may hold values from -0.75 to 0.75
- w_dst: bfloat16 [64, 256], replicated, may hold values from -0.75 to 0.75
- species_src: bfloat16 [4, 256], replicated, may hold values from -3 to 3
- species_dst: bfloat16 [4, 256], replicated, may hold values from -3 to 3
- w_hidden: bfloat16 [256, 256], replicated, may hold values from -0.375 to 0.375
- w_latent: bfloat16 [256, 64], replicated, may hold values from -0.375 to 0.375
- w_energy: float32 [64], replicated, may hold values from -0.75 to 0.75
Outputs:
- energy: float32 [1], replicated
- forces: float32 [3, 65536], P(None, ('gx', 'gy'))
- feature_grads: float32 [64, 65536], P(None, ('gx', 'gy'))
Inputs may be any that keep to these rules, and one draw needn't show every extreme that they name: `local_pairs`: rows 0 and 1 are different atoms of the block, below 2048; rows 2 and 3 are species below 4. `cross_x`: row 0 an atom below 2048, row 1 a slot below 1536, rows 2 and 3 species below 4. `cross_y`: row 0 an atom below 2048, row 1 a slot below 1536, rows 2 and 3 species below 4. `pair_counts`: column 0 counts live slots of local_pairs (at most 6144), columns 1 and 2 those of cross_x and cross_y (at most 2048); live slots come first; some device is full in each column.
All inputs are finite; a program needn't handle non-finite values.
Results may differ from a plain program's by a relative error of at most 0.0095.
Values may be sent and summed in bfloat16 or wider, within the bound.
No kernel may reach another device: no remote copies, remote signals or barrier semaphores. Data moves between devices by JAX's collectives and lax.ppermute only.
A program may use at most 64 MiB of HBM per device.

v0:
```python
import jax
import jax.numpy as jnp
from jax import lax
from jax.sharding import PartitionSpec as P

BLOCK = 512
cutoff_radius = 6.0
block_edge = 6.0
softening = 0.1


def shifted(array, axis, by):
    length = lax.axis_size(axis)
    return lax.ppermute(array, axis, [(i, (i + by) % length) for i in range(length)])


def pair_energy(
    src_pos, src_feat, dst_pos, dst_feat, spec_src, spec_dst, live_mask, offset, weights
):
    w_rbf, w_src, w_dst, species_src, species_dst, w_hidden, w_latent, w_energy = weights
    displace = dst_pos + offset[:, None] - src_pos
    radius = jnp.sqrt(jnp.sum(displace * displace, axis=0) + softening)
    orders = jnp.arange(1, w_rbf.shape[0] + 1).astype(jnp.float32)[:, None]
    basis = (jnp.sin(orders * (jnp.pi / cutoff_radius) * radius[None, :]) / radius[None, :]).astype(
        jnp.bfloat16
    )
    kinds = jnp.arange(species_src.shape[0], dtype=jnp.int32)[:, None]
    onehot_src = (spec_src[None, :] == kinds).astype(jnp.bfloat16)
    onehot_dst = (spec_dst[None, :] == kinds).astype(jnp.bfloat16)
    pre = jnp.dot(w_rbf.T, basis, preferred_element_type=jnp.float32)
    pre = pre + jnp.dot(w_src.T, src_feat.astype(jnp.bfloat16), preferred_element_type=jnp.float32)
    pre = pre + jnp.dot(w_dst.T, dst_feat.astype(jnp.bfloat16), preferred_element_type=jnp.float32)
    pre = pre + jnp.dot(species_src.T, onehot_src, preferred_element_type=jnp.float32)
    pre = pre + jnp.dot(species_dst.T, onehot_dst, preferred_element_type=jnp.float32)
    hidden = jax.nn.silu(pre).astype(jnp.bfloat16)
    second = jax.nn.silu(jnp.dot(w_hidden.T, hidden, preferred_element_type=jnp.float32)).astype(
        jnp.bfloat16
    )
    latent = jnp.dot(w_latent.T, second, preferred_element_type=jnp.float32)
    ratio = jnp.minimum(radius / cutoff_radius, 1.0)
    envelope = (1.0 - ratio**2) ** 2
    scores = jnp.dot(w_energy, latent, precision=lax.Precision.HIGHEST)
    return jnp.sum(envelope * scores * live_mask)


def block_grads(
    src_pos, src_feat, dst_pos, dst_feat, spec_src, spec_dst, live_mask, offset, weights
):

    def energy_of(pos_one, feat_one, pos_two, feat_two):
        return pair_energy(
            pos_one, feat_one, pos_two, feat_two, spec_src, spec_dst, live_mask, offset, weights
        )

    energy, pullback = jax.vjp(
        energy_of, src_pos, src_feat.astype(jnp.float32), dst_pos, dst_feat.astype(jnp.float32)
    )
    return (energy, pullback(jnp.ones_like(energy)))


def run_edges(
    src_pos, src_feat, dst_pos, dst_feat, spec_src, spec_dst, live_mask, live_count, offset, weights
):
    inputs = (src_pos, src_feat, dst_pos, dst_feat, spec_src, spec_dst, live_mask)
    edges = src_pos.shape[1]
    filled = (live_count + BLOCK - 1) // BLOCK
    start_grads = (
        jnp.zeros((3, edges), jnp.float32),
        jnp.zeros((src_feat.shape[0], edges), jnp.float32),
        jnp.zeros((3, edges), jnp.float32),
        jnp.zeros((dst_feat.shape[0], edges), jnp.float32),
    )

    def visit_live(index, carry):
        total, grads = carry
        begin = index * BLOCK
        blocks = tuple(
            (lax.dynamic_slice_in_dim(item, begin, BLOCK, axis=item.ndim - 1) for item in inputs)
        )
        energy, parts = block_grads(*blocks, offset, weights)
        grads = tuple(
            (
                lax.dynamic_update_slice_in_dim(whole, piece, begin, axis=1)
                for whole, piece in zip(grads, parts)
            )
        )
        return (total + energy, grads)

    return lax.fori_loop(0, filled, visit_live, (jnp.zeros((), jnp.float32), start_grads))


def on_device(
    positions,
    features,
    halo_lists,
    local_pairs,
    cross_x,
    cross_y,
    pair_counts,
    w_rbf,
    w_src,
    w_dst,
    species_src,
    species_dst,
    w_hidden,
    w_latent,
    w_energy,
):
    weights = (w_rbf, w_src, w_dst, species_src, species_dst, w_hidden, w_latent, w_energy)
    atoms = positions.shape[1]
    halo_size = halo_lists.shape[1]
    width = features.shape[0]
    list_x = halo_lists[0]
    list_y = halo_lists[1]
    got_pos_x = shifted(positions[:, list_x], "gx", -1)
    got_feat_x = shifted(features[:, list_x], "gx", -1)
    got_pos_y = shifted(positions[:, list_y], "gy", -1)
    got_feat_y = shifted(features[:, list_y], "gy", -1)
    zero_off = jnp.zeros((3,), jnp.float32)
    off_x = jnp.array([block_edge, 0.0, 0.0], jnp.float32)
    off_y = jnp.array([0.0, block_edge, 0.0], jnp.float32)
    counts = pair_counts[0]
    slots_loc = jnp.arange(local_pairs.shape[1], dtype=jnp.int32)
    slots_cross = jnp.arange(cross_x.shape[1], dtype=jnp.int32)
    live_loc = (slots_loc < counts[0]).astype(jnp.float32)
    flag_x = (slots_cross < counts[1]).astype(jnp.int32)
    flag_y = (slots_cross < counts[2]).astype(jnp.int32)
    source, target = (local_pairs[0], local_pairs[1])
    energy_loc, grads = run_edges(
        positions[:, source],
        features[:, source],
        positions[:, target],
        features[:, target],
        local_pairs[2],
        local_pairs[3],
        live_loc,
        counts[0],
        zero_off,
        weights,
    )
    grad_pos = (
        jnp.zeros((3, atoms), jnp.float32).at[:, source].add(grads[0]).at[:, target].add(grads[2])
    )
    grad_feat = (
        jnp.zeros((width, atoms), jnp.float32)
        .at[:, source]
        .add(grads[1])
        .at[:, target]
        .add(grads[3])
    )
    source_x, slot_x = (cross_x[0], cross_x[1])
    src_pos_x = positions[:, source_x]
    src_feat_x = features[:, source_x]
    energy_x, grads_x = run_edges(
        src_pos_x,
        src_feat_x,
        got_pos_x[:, slot_x],
        got_feat_x[:, slot_x],
        cross_x[2],
        cross_x[3],
        flag_x.astype(jnp.float32),
        counts[1],
        off_x,
        weights,
    )
    grad_pos = grad_pos.at[:, source_x].add(grads_x[0])
    grad_feat = grad_feat.at[:, source_x].add(grads_x[1])
    source_y, slot_y = (cross_y[0], cross_y[1])
    src_pos_y = positions[:, source_y]
    src_feat_y = features[:, source_y]
    energy_y, grads_y = run_edges(
        src_pos_y,
        src_feat_y,
        got_pos_y[:, slot_y],
        got_feat_y[:, slot_y],
        cross_y[2],
        cross_y[3],
        flag_y.astype(jnp.float32),
        counts[2],
        off_y,
        weights,
    )
    grad_pos = grad_pos.at[:, source_y].add(grads_y[0])
    grad_feat = grad_feat.at[:, source_y].add(grads_y[1])
    lent_pos_x = jnp.zeros((3, halo_size), jnp.float32).at[:, slot_x].add(grads_x[2])
    lent_feat_x = jnp.zeros((width, halo_size), jnp.float32).at[:, slot_x].add(grads_x[3])
    back_pos_x, back_feat_x = shifted((lent_pos_x, lent_feat_x), "gx", 1)
    lent_pos_y = jnp.zeros((3, halo_size), jnp.float32).at[:, slot_y].add(grads_y[2])
    lent_feat_y = jnp.zeros((width, halo_size), jnp.float32).at[:, slot_y].add(grads_y[3])
    back_pos_y, back_feat_y = shifted((lent_pos_y, lent_feat_y), "gy", 1)
    grad_pos = grad_pos.at[:, list_x].add(back_pos_x).at[:, list_y].add(back_pos_y)
    grad_feat = grad_feat.at[:, list_x].add(back_feat_x).at[:, list_y].add(back_feat_y)
    total = lax.psum(energy_loc + energy_x + energy_y, ("gx", "gy"))
    atoms_all = atoms * lax.axis_size("gx") * lax.axis_size("gy")
    energy = (total / atoms_all).reshape(1)
    return (energy, -grad_pos, grad_feat)


def solution(mesh):
    return jax.shard_map(
        on_device,
        mesh=mesh,
        in_specs=(
            P(None, ("gx", "gy")),
            P(None, ("gx", "gy")),
            P(None, ("gx", "gy")),
            P(None, ("gx", "gy")),
            P(None, ("gx", "gy")),
            P(None, ("gx", "gy")),
            P(("gx", "gy"), None),
            P(),
            P(),
            P(),
            P(),
            P(),
            P(),
            P(),
            P(),
        ),
        out_specs=(P(), P(None, ("gx", "gy")), P(None, ("gx", "gy"))),
        check_vma=False,
    )
```

profile of v0, /device:TPU:0, one launch (start us, length us, event | category | flops | bytes accessed | tf_op | source)
XLA Modules:
  0.0 767.4 jit_solution(1176307451014661208)
XLA Ops:
  2.7 2.6 gather_fusion.4
  5.5 5.5 collective-permute-start
  11.3 4.0 gather_fusion.8
  16.1 2.6 gather_fusion.10
  19.5 1.5 collective-permute-start.2
  21.0 4.0 gather_fusion.14
  31.0 20.9 %gather_fusion.1 = f32[6144,3]{1,0:T(8,128)} fusion(f32[3,2048]{0,1:T(8,128)S(1)} %copy.112, s32[6144]{0:T(1024)S(1)} %broadcast_clamp_fusion), kind=kCustom, calls=%fused_computation.1 | custom fusion | bytes 172032 | tf_op jit(solution)/shard_map/gather | solution.py:130
  51.9 22.1 %gather_fusion.2 = bf16[6144,64]{1,0:T(8,128)(2,1)} fusion(bf16[64,2048]{0,1:T(8,128)(2,1)S(1)} %copy.114, s32[6144]{0:T(1024)S(1)} %broadcast_clamp_fusion), kind=kCustom, calls=%fused_computation.2 | custom fusion | bytes 1597440 | tf_op jit(solution)/shard_map/gather | solution.py:131
  74.0 20.9 %gather_fusion = f32[6144,3]{1,0:T(8,128)} fusion(f32[3,2048]{0,1:T(8,128)S(1)} %copy.112, s32[6144]{0:T(1024)S(1)} %broadcast_clamp_fusion.1), kind=kCustom, calls=%fused_computation | custom fusion | bytes 172032 | tf_op jit(solution)/shard_map/gather | solution.py:132
  94.9 22.0 %gather_fusion.3 = bf16[6144,64]{1,0:T(8,128)(2,1)} fusion(bf16[64,2048]{0,1:T(8,128)(2,1)S(1)} %copy.114, s32[6144]{0:T(1024)S(1)} %broadcast_clamp_fusion.1), kind=kCustom, calls=%fused_computation.3 | custom fusion | bytes 1597440 | tf_op jit(solution)/shard_map/gather | solution.py:133
  117.6 7.6 gather_fusion.6
  125.2 6.2 gather_fusion.7
  132.0 7.6 gather_fusion.12
  139.6 8.0 %gather_fusion.13 = bf16[2048,64]{1,0:T(8,128)(2,1)} fusion(bf16[64,2048]{0,1:T(8,128)(2,1)S(1)} %copy.114, s32[2048]{0:T(1024)S(1)} %broadcast_clamp_fusion.4), kind=kCustom, calls=%fused_computation.13 | custom fusion | bytes 532480 | tf_op jit(solution)/shard_map/gather | solution.py:170
  147.6 3.0 copy.116
  150.6 3.1 copy.117
  153.7 1.4 copy.118
  155.1 2.5 copy.119
  158.2 1.6 copy.145
  160.3 7.6 gather_fusion.5
  167.9 1.6 copy.130
  169.8 7.6 gather_fusion.11
  177.4 1.6 copy.144
  179.0 6.2 gather_fusion.9
  185.6 17.9 %while.57 = (s32[]{:T(128)}, f32[]{:T(128)}, f32[3,2048]{1,0:T(4,128)S(1)}, f32[64,2048]{1,0:T(8,128)S(1)}, f32[3,2048]{1,0:T(4,128)S(1)}, /*index=5*/f32[64,204...) while((s32[]{:T(128)}, f32[]{:T(128)}, ...), condition=%wide.region_11.12_spmd.clone, body=%wide.region_6.11_spmd.sunk.clone.sunk | while | flops 246594080 | bytes 9612223 | solution.py:89
  187.5 2.0 convolution_bitcast_fusion.14
  189.5 1.6 fusion.370
  196.4 2.0 convolution_bitcast_fusion.14
  198.4 1.6 fusion.370
  203.5 6.2 gather_fusion.15
  210.1 20.8 %while.58 = (s32[]{:T(128)}, f32[]{:T(128)}, f32[3,2048]{1,0:T(4,128)S(1)}, f32[64,2048]{1,0:T(8,128)S(1)}, f32[3,2048]{1,0:T(4,128)S(1)}, /*index=5*/f32[64,204...) while((s32[]{:T(128)}, f32[]{:T(128)}, ...), condition=%wide.region_17.18_spmd.clone, body=%wide.region_12.17_spmd.sunk.clone.sunk | while | flops 246594080 | bytes 9743323 | solution.py:89
  213.5 2.0 convolution_bitcast_fusion.16
  215.5 1.6 fusion.400
  223.8 2.0 convolution_bitcast_fusion.16
  225.8 1.6 fusion.400
  232.2 12.0 %scatter_custom_fusion.12 = f32[64,1536]{0,1:T(8,128)S(1)} fusion(s32[2048]{0:T(1024)} %bitcast.415, f32[2048,64]{1,0:T(8,128)} %copy.162, f32[]{:T(128)} %constant.142.clone.1), kind=kCustom, calls=%fused_computation.275 | custom fusion | flops 131072 | bytes 393728 | tf_op jit(solution)/shard_map/scatter-add | solution.py:186
  245.3 10.9 %collective-permute-start.6 = (f32[64,1536]{1,0:T(8,128)}, f32[64,1536]{1,0:T(8,128)}, u32[]{:S(2)}, u32[]{:S(2)}) collective-permute-start(f32[64,1536]{1,0:T(8,128)} %copy.163), channel_id=1, source_target_pairs={{0,2},{2,4},{4,6},{6,8},{8,10},{10,12},{12,14},{14,16},{16,18},{18... | collective-permute-start | bytes 1179656 | tf_op jit(solution)/shard_map/ppermute | solution.py:14
  256.5 11.8 %scatter_custom_fusion.14 = f32[64,1536]{0,1:T(8,128)S(1)} fusion(s32[2048]{0:T(1024)} %bitcast.412, f32[2048,64]{1,0:T(8,128)S(1)} %copy.165, f32[]{:T(128)} %constant.142.clone.1), kind=kCustom, calls=%fused_computation.273 | custom fusion | flops 131072 | bytes 393728 | tf_op jit(solution)/shard_map/scatter-add | solution.py:189
  269.7 11.8 %scatter_custom_fusion.4 = f32[3,1536]{0,1:T(8,128)S(1)} fusion(s32[2048]{0:T(1024)} %bitcast.416, f32[2048,3]{1,0:T(8,128)S(1)} %copy.152, f32[]{:T(128)} %constant.142.clone.1), kind=kCustom, calls=%fused_computation.279 | custom fusion | flops 6144 | bytes 18944 | tf_op jit(solution)/shard_map/scatter-add | solution.py:185
  282.4 26.4 %collective-permute-start.4 = (f32[3,1536]{1,0:T(4,128)}, f32[3,1536]{1,0:T(4,128)}, u32[]{:S(2)}, u32[]{:S(2)}) collective-permute-start(f32[3,1536]{1,0:T(4,128)} %copy.153), channel_id=1, source_target_pairs={{0,2},{2,4},{4,6},{6,8},{8,10},{10,12},{12,14},{14,16},{16,18},{18... | collective-permute-start | bytes 55304 | tf_op jit(solution)/shard_map/ppermute | solution.py:14
  309.1 11.8 %scatter_custom_fusion.6 = f32[3,1536]{0,1:T(8,128)S(1)} fusion(s32[2048]{0:T(1024)} %bitcast.413, f32[2048,3]{1,0:T(8,128)S(1)} %copy.155, f32[]{:T(128)} %constant.142.clone.1), kind=kCustom, calls=%fused_computation.277 | custom fusion | flops 6144 | bytes 18944 | tf_op jit(solution)/shard_map/scatter-add | solution.py:188
  323.5 40.1 %while.56 = (s32[]{:T(128)}, f32[]{:T(128)}, f32[3,6144]{1,0:T(4,128)S(1)}, f32[64,6144]{1,0:T(8,128)S(1)}, f32[3,6144]{1,0:T(4,128)S(1)}, /*index=5*/f32[64,614...) while((s32[]{:T(128)}, f32[]{:T(128)}, ...), condition=%wide.region_5.6_spmd, body=%wide.region_0.5_spmd.sunk | while | flops 246594080 | bytes 9610155 | solution.py:89
  331.1 1.4 fusion.340
  344.4 1.4 fusion.340
  357.7 1.4 fusion.340
  363.6 2.3 copy.158
  365.9 2.2 copy.159
  368.1 2.2 copy.148
  370.3 2.2 copy.149
  372.5 33.7 %scatter_custom_fusion.8 = f32[64,2048]{0,1:T(8,128)S(1)} fusion(s32[6144]{0:T(1024)} %bitcast.403, f32[6144,64]{1,0:T(8,128)} %copy.158, f32[]{:T(128)} %constant.142.clone.1), kind=kCustom, calls=%fused_computation.269 | custom fusion | flops 393216 | bytes 524800 | tf_op jit(solution)/shard_map/scatter-add | solution.py:147
  406.3 33.9 %scatter_fusion.5 = f32[64,2048]{0,1:T(8,128)S(1)} fusion(f32[64,2048]{0,1:T(8,128)S(1)} %scatter_custom_fusion.8, s32[6144]{0:T(1024)S(1)} %bitcast.387, f32[6144,64]{1,0:T(8,128)} %copy.159), kind=kCustom, calls=%fused_computation.25 | custom fusion | flops 393216 | bytes 4743168 | tf_op jit(solution)/shard_map/scatter-add | solution.py:149
  440.2 33.7 %scatter_custom_fusion = f32[3,2048]{0,1:T(8,128)S(1)} fusion(s32[6144]{0:T(1024)} %bitcast.404, f32[6144,3]{1,0:T(8,128)} %copy.148, f32[]{:T(128)} %constant.142.clone.1), kind=kCustom, calls=%fused_computation.271 | custom fusion | flops 18432 | bytes 25088 | tf_op jit(solution)/shard_map/scatter-add | solution.py:142
  473.9 33.9 %scatter_fusion = f32[3,2048]{0,1:T(8,128)S(1)} fusion(f32[3,2048]{0,1:T(8,128)S(1)} %scatter_custom_fusion, s32[6144]{0:T(1024)S(1)} %bitcast.388, f32[6144,3]{1,0:T(8,128)} %copy.149), kind=kCustom, calls=%fused_computation.17 | custom fusion | flops 18432 | bytes 245760 | tf_op jit(solution)/shard_map/scatter-add | solution.py:142
  507.8 157.6 %psum.7 = f32[]{:T(128)} all-reduce(f32[]{:T(128)S(6)} %add.371), channel_id=1, replica_groups=mesh['gx'=16,'gy'=2] {'gx','gy'}, use_global_device_ids=true, to_apply=%region_18.19 | all-reduce | flops 1 | bytes 8 | tf_op jit(solution)/shard_map/psum | solution.py:193
  666.8 2.4 copy.161
  672.0 11.9 %scatter_fusion.6 = f32[64,2048]{0,1:T(8,128)S(1)} fusion(f32[64,2048]{0,1:T(8,128)S(1)} %scatter_fusion.5, s32[2048]{0:T(1024)S(1)} %bitcast.393, f32[2048,64]{1,0:T(8,128)S(1)} %copy.160), kind=kCustom, calls=%fused_computation.26 | custom fusion | flops 131072 | bytes 1581056 | tf_op jit(solution)/shard_map/scatter-add | solution.py:167
  683.8 12.2 %scatter_fusion.7 = f32[64,2048]{0,1:T(8,128)S(1)} fusion(f32[64,2048]{0,1:T(8,128)S(1)} %scatter_fusion.6, s32[2048]{0:T(1024)S(1)} %bitcast.396, f32[2048,64]{1,0:T(8,128)} %copy.161), kind=kCustom, calls=%fused_computation.27 | custom fusion | flops 131072 | bytes 1581056 | tf_op jit(solution)/shard_map/scatter-add | solution.py:184
  696.1 12.2 %scatter_fusion.1 = f32[3,2048]{0,1:T(8,128)S(1)} fusion(f32[3,2048]{0,1:T(8,128)S(1)} %scatter_fusion, s32[2048]{0:T(1024)S(1)} %bitcast.394, f32[2048,3]{1,0:T(8,128)} %copy.150), kind=kCustom, calls=%fused_computation.18 | custom fusion | flops 6144 | bytes 81920 | tf_op jit(solution)/shard_map/scatter-add | solution.py:166
  708.3 12.2 %scatter_fusion.2 = f32[3,2048]{0,1:T(8,128)S(1)} fusion(f32[3,2048]{0,1:T(8,128)S(1)} %scatter_fusion.1, s32[2048]{0:T(1024)S(1)} %bitcast.397, f32[2048,3]{1,0:T(8,128)} %copy.151), kind=kCustom, calls=%fused_computation.19 | custom fusion | flops 6144 | bytes 81920 | tf_op jit(solution)/shard_map/scatter-add | solution.py:183
  722.3 1.9 copy.157
  724.2 9.1 %scatter_fusion.3 = f32[3,2048]{0,1:T(8,128)S(1)} fusion(f32[3,2048]{0,1:T(8,128)S(1)} %scatter_fusion.2, s32[1536]{0:T(1024)S(1)} %get-tuple-element.733, f32[1536,3]{1,0:T(8,128)S(1)} %copy.154), kind=kCustom, calls=%fused_computation.21 | custom fusion | flops 4608 | bytes 61440 | tf_op jit(solution)/shard_map/scatter-add | solution.py:191
  733.3 9.7 %scatter_fusion.4 = f32[3,2048]{0,1:T(8,128)S(1)} fusion(f32[3,2048]{0,1:T(8,128)S(1)} %scatter_fusion.3, s32[1536]{0:T(1024)S(1)} %get-tuple-element.732, f32[1536,3]{1,0:T(8,128)} %copy.157), kind=kCustom, calls=%fused_computation.23 | custom fusion | flops 4608 | bytes 61440 | tf_op jit(solution)/shard_map/scatter-add | solution.py:191
  746.6 9.1 %scatter_fusion.8 = f32[64,2048]{0,1:T(8,128)S(1)} fusion(f32[64,2048]{0,1:T(8,128)S(1)} %scatter_fusion.7, s32[1536]{0:T(1024)S(1)} %get-tuple-element.733, f32[1536,64]{1,0:T(8,128)S(1)} %copy.164), kind=kCustom, calls=%fused_computation.29 | custom fusion | flops 98304 | bytes 1185792 | tf_op jit(solution)/shard_map/scatter-add | solution.py:192
  755.8 9.1 %scatter_fusion.9 = f32[64,2048]{0,1:T(8,128)S(1)} fusion(f32[64,2048]{0,1:T(8,128)S(1)} %scatter_fusion.8, s32[1536]{0:T(1024)S(1)} %get-tuple-element.732, f32[1536,64]{1,0:T(8,128)S(1)} %copy.167), kind=kCustom, calls=%fused_computation.31 | custom fusion | flops 98304 | bytes 1185792 | tf_op jit(solution)/shard_map/scatter-add | solution.py:192
  (254 shorter events, 83.9 us)
Async XLA Ops:
  0.6 10.4 %copy-start.11 = (bf16[64,2048]{1,0:T(8,128)(2,1)S(1)}, bf16[64,2048]{1,0:T(8,128)(2,1)}, u32[]{:S(2)}) copy-start(bf16[64,2048]{1,0:T(8,128)(2,1)} %param.24) | copy-start | bytes 786436
  5.5 154.5 %collective-permute-start = (f32[3,1536]{1,0:T(4,128)S(1)}, f32[3,1536]{1,0:T(4,128)S(1)}, u32[]{:S(2)}, u32[]{:S(2)}) collective-permute-start(f32[3,1536]{1,0:T(4,128)S(1)} %copy.121), channel_id=1, source_target_pairs={{0,30},{2,0},{4,2},{6,4},{8,6},{10,8},{12,10},{14,12},{16,14},{18,... | collective-permute-start | bytes 55304 | tf_op jit(solution)/shard_map/ppermute | solution.py:14
  15.3 10.2 %copy-start.19 = (s32[4,6144]{1,0:T(4,128)S(1)}, s32[4,6144]{1,0:T(4,128)}, u32[]{:S(2)}) copy-start(s32[4,6144]{1,0:T(4,128)} %param.26) | copy-start | bytes 294916
  15.3 11.0 %copy-start.21 = (s32[4,2048]{1,0:T(4,128)S(1)}, s32[4,2048]{1,0:T(4,128)}, u32[]{:S(2)}) copy-start(s32[4,2048]{1,0:T(4,128)} %param.27) | copy-start | bytes 98308
  15.3 11.0 %copy-start.22 = (s32[4,2048]{1,0:T(4,128)S(1)}, s32[4,2048]{1,0:T(4,128)}, u32[]{:S(2)}) copy-start(s32[4,2048]{1,0:T(4,128)} %param.28) | copy-start | bytes 98308
  15.3 163.6 %collective-permute-start.1 = (bf16[64,1536]{0,1:T(8,128)(2,1)}, bf16[64,1536]{0,1:T(8,128)(2,1)S(1)}, u32[]{:S(2)}, u32[]{:S(2)}) collective-permute-start(bf16[64,1536]{0,1:T(8,128)(2,1)} %bitcast.32), channel_id=1, source_target_pairs={{0,30},{2,0},{4,2},{6,4},{8,6},{10,8},{12,10},{14,12},{16,14},{18,... | collective-permute-start | bytes 589832 | tf_op jit(solution)/shard_map/ppermute | solution.py:14
  16.1 11.0 %copy-start.26 = (s32[1,3]{1,0:T(1,128)S(1)}, s32[1,3]{1,0:T(1,128)}, u32[]{:S(2)}) copy-start(s32[1,3]{1,0:T(1,128)} %param.29) | copy-start | bytes 40
  19.5 149.9 %collective-permute-start.2 = (f32[3,1536]{1,0:T(4,128)}, f32[3,1536]{1,0:T(4,128)S(1)}, u32[]{:S(2)}, u32[]{:S(2)}) collective-permute-start(f32[3,1536]{1,0:T(4,128)} %copy.135), channel_id=1, source_target_pairs={{0,1},{1,0},{2,3},{3,2},{4,5},{5,4},{6,7},{7,6},{8,9},{9,8},{10,11... | collective-permute-start | bytes 55304 | tf_op jit(solution)/shard_map/ppermute | solution.py:14
  25.0 178.5 %collective-permute-start.3 = (bf16[64,1536]{0,1:T(8,128)(2,1)}, bf16[64,1536]{0,1:T(8,128)(2,1)S(1)}, u32[]{:S(2)}, u32[]{:S(2)}) collective-permute-start(bf16[64,1536]{0,1:T(8,128)(2,1)} %bitcast.46), channel_id=1, source_target_pairs={{0,1},{1,0},{2,3},{3,2},{4,5},{5,4},{6,7},{7,6},{8,9},{9,8},{10,11... | collective-permute-start | bytes 589832 | tf_op jit(solution)/shard_map/ppermute | solution.py:14
  25.6 48.4 %copy-start.20 = (s32[6144,1]{0,1:T(1,128)}, s32[6144,1]{0,1:T(1,128)S(1)}, u32[]{:S(2)}) copy-start(s32[6144,1]{0,1:T(1,128)S(1)} %get-tuple-element.893) | copy-start | bytes 73732
  26.3 47.7 %copy-start.24 = (s32[2048,1]{0,1:T(1,128)}, s32[2048,1]{0,1:T(1,128)S(1)}, u32[]{:S(2)}) copy-start(s32[2048,1]{0,1:T(1,128)S(1)} %get-tuple-element.902) | copy-start | bytes 24580
  26.4 2.6 copy-start.23
  150.6 3.1 copy-start.3
  155.1 2.5 copy-start.7
  157.6 2.1 copy-start.6
  178.9 6.6 copy-start
  178.9 6.6 copy-start.1
  178.9 6.6 copy-start.8
  178.9 6.6 copy-start.9
  178.9 6.6 copy-start.10
  178.9 6.6 copy-start.18
  179.0 6.6 copy-start.25
  179.0 6.6 copy-start.27
  203.5 6.2 copy-start.12
  203.5 6.4 copy-start.4
  213.2 2.3 copy-start.28
  223.5 2.3 copy-start.28
  230.8 14.4 %copy-start.5 = (f32[64,2048]{1,0:T(8,128)}, f32[64,2048]{1,0:T(8,128)S(1)}, u32[]{:S(2)}) copy-start(f32[64,2048]{1,0:T(8,128)S(1)} %get-tuple-element.376) | copy-start | bytes 1572868
  230.8 14.4 %copy-start.14 = (f32[3,2048]{1,0:T(4,128)}, f32[3,2048]{1,0:T(4,128)S(1)}, u32[]{:S(2)}) copy-start(f32[3,2048]{1,0:T(4,128)S(1)} %get-tuple-element.370) | copy-start | bytes 73732
  230.9 14.4 %copy-start.16 = (f32[3,2048]{1,0:T(4,128)}, f32[3,2048]{1,0:T(4,128)S(1)}, u32[]{:S(2)}) copy-start(f32[3,2048]{1,0:T(4,128)S(1)} %get-tuple-element.372) | copy-start | bytes 73732
  245.3 498.8 %collective-permute-start.6 = (f32[64,1536]{1,0:T(8,128)}, f32[64,1536]{1,0:T(8,128)}, u32[]{:S(2)}, u32[]{:S(2)}) collective-permute-start(f32[64,1536]{1,0:T(8,128)} %copy.163), channel_id=1, source_target_pairs={{0,2},{2,4},{4,6},{6,8},{8,10},{10,12},{12,14},{14,16},{16,18},{18... | collective-permute-start | bytes 1179656 | tf_op jit(solution)/shard_map/ppermute | solution.py:14
  256.2 13.1 %copy-start.13 = (f32[3,2048]{1,0:T(4,128)S(1)}, f32[3,2048]{1,0:T(4,128)}, u32[]{:S(2)}) copy-start(f32[3,2048]{1,0:T(4,128)} %copy-done.12) | copy-start | bytes 73732
  269.3 39.4 %copy-start.17 = (f32[3,2048]{1,0:T(4,128)S(1)}, f32[3,2048]{1,0:T(4,128)}, u32[]{:S(2)}) copy-start(f32[3,2048]{1,0:T(4,128)} %copy-done.16) | copy-start | bytes 73732
  269.3 476.0 %collective-permute-start.7 = (f32[64,1536]{1,0:T(8,128)}, f32[64,1536]{1,0:T(8,128)}, u32[]{:S(2)}, u32[]{:S(2)}) collective-permute-start(f32[64,1536]{1,0:T(8,128)} %copy.166), channel_id=1, source_target_pairs={{0,1},{1,0},{2,3},{3,2},{4,5},{5,4},{6,7},{7,6},{8,9},{9,8},{10,11... | collective-permute-start | bytes 1179656 | tf_op jit(solution)/shard_map/ppermute | solution.py:14
  282.4 438.9 %collective-permute-start.4 = (f32[3,1536]{1,0:T(4,128)}, f32[3,1536]{1,0:T(4,128)}, u32[]{:S(2)}, u32[]{:S(2)}) collective-permute-start(f32[3,1536]{1,0:T(4,128)} %copy.153), channel_id=1, source_target_pairs={{0,2},{2,4},{4,6},{6,8},{8,10},{10,12},{12,14},{14,16},{16,18},{18... | collective-permute-start | bytes 55304 | tf_op jit(solution)/shard_map/ppermute | solution.py:14
  321.7 400.5 %collective-permute-start.5 = (f32[3,1536]{1,0:T(4,128)}, f32[3,1536]{1,0:T(4,128)}, u32[]{:S(2)}, u32[]{:S(2)}) collective-permute-start(f32[3,1536]{1,0:T(4,128)} %copy.156), channel_id=1, source_target_pairs={{0,1},{1,0},{2,3},{3,2},{4,5},{5,4},{6,7},{7,6},{8,9},{9,8},{10,11... | collective-permute-start | bytes 55304 | tf_op jit(solution)/shard_map/ppermute | solution.py:14
  322.0 1.4 copy-start.29
  363.6 2.3 copy-start.2
  666.8 3.8 copy-start.15
where the time goes:
time: 780 us; the launch traced here: 767 us
  other arithmetic  287 us (37%)
  local copies, waits for them, and re-layouts  214 us (27%)
  blocking collectives  158 us (20%)
  matrix products  51.4 us (7%)
  starting transfers between devices  45.8 us (6%)
    psum x1, blocking collectives, on_device(): total = lax.psum(energy_loc + energy_x + energy_y, ('gx', 'gy'))  158 us
    scatter-add x2, other arithmetic, on_device(): jnp.zeros((3, atoms), jnp.float32).at[:, source].add(grads[0]).at[:, target]  67.6 us
    scatter-add x2, other arithmetic, on_device(): grad_feat = jnp.zeros((width, atoms), jnp.float32).at[:, source].add(grad...  67.6 us
    ppermute x8, starting transfers between devices, shifted(): lax.ppermute(array, axis, [(i, (i + by) % length) for i in range(length)])  45.8 us
    while x16, local copies, waits for them, and re-layouts, run_edges(): lax.fori_loop(0, filled, visit_live, (jnp.zeros((), jnp.float32), start_g...  27.8 us
    dot_general x14, matrix products, pair_energy(): jnp.dot(w_hidden.T, hidden, preferred_element_type=jnp.float32)  22.1 us
    gather x1, local copies, waits for them, and re-layouts, on_device(): features[:, source]  22.1 us
    gather x1, local copies, waits for them, and re-layouts, on_device(): features[:, target]  22 us
  transfers between devices with their start and end apart: 8, of which 0 were waited for; matrix products, arithmetic and copies ran while one was open for 64% of the time, Pallas kernels for 0%

commit v1 on v0

--- a/solution.py
+++ b/solution.py
@@ -190,7 +190,7 @@
     back_pos_y, back_feat_y = shifted((lent_pos_y, lent_feat_y), "gy", 1)
     grad_pos = grad_pos.at[:, list_x].add(back_pos_x).at[:, list_y].add(back_pos_y)
     grad_feat = grad_feat.at[:, list_x].add(back_feat_x).at[:, list_y].add(back_feat_y)
-    total = lax.psum(energy_loc + energy_x + energy_y, ("gx", "gy"))
+    total = lax.psum(lax.psum(energy_loc + energy_x + energy_y, "gy"), "gx")
     atoms_all = atoms * lax.axis_size("gx") * lax.axis_size("gy")
     energy = (total / atoms_all).reshape(1)
     return (energy, -grad_pos, grad_feat)

time: 780 us -> 773 us (level)
  blocking collectives: 158 us -> 150 us
    psum x1 -> x2, blocking collectives: 158 us -> 150 us  [on_device(): total = lax.psum(lax.psum(energy_loc + energy_x + energy_y, 'gy'), 'gx')]
where the time goes in v1:
time: 773 us; the launch traced here: 760 us
  other arithmetic  288 us (37%)
  local copies, waits for them, and re-layouts  214 us (28%)
  blocking collectives  150 us (19%)
  matrix products  51.4 us (7%)
  starting transfers between devices  45.8 us (6%)
    psum x2, blocking collectives, on_device(): total = lax.psum(lax.psum(energy_loc + energy_x + energy_y, 'gy'), 'gx')  150 us
    scatter-add x2, other arithmetic, on_device(): grad_feat = jnp.zeros((width, atoms), jnp.float32).at[:, source].add(grad...  67.6 us
    scatter-add x2, other arithmetic, on_device(): jnp.zeros((3, atoms), jnp.float32).at[:, source].add(grads[0]).at[:, target]  67.6 us
    ppermute x8, starting transfers between devices, shifted(): lax.ppermute(array, axis, [(i, (i + by) % length) for i in range(length)])  45.8 us
    while x16, local copies, waits for them, and re-layouts, run_edges(): lax.fori_loop(0, filled, visit_live, (jnp.zeros((), jnp.float32), start_g...  27.8 us
    dot_general x14, matrix products, pair_energy(): jnp.dot(w_hidden.T, hidden, preferred_element_type=jnp.float32)  22.1 us
    gather x1, local copies, waits for them, and re-layouts, on_device(): features[:, source]  22.1 us
    gather x1, local copies, waits for them, and re-layouts, on_device(): features[:, target]  22 us
  transfers between devices with their start and end apart: 8, of which 0 were waited for; matrix products, arithmetic and copies ran while one was open for 64% of the time, Pallas kernels for 0%

profile of v1, /device:TPU:0, one launch (start us, length us, event | category | flops | bytes accessed | tf_op | source)
XLA Modules:
  0.0 760.4 jit_solution(16097306824922658178)
XLA Ops:
  2.7 2.6 gather_fusion.4
  5.5 5.5 collective-permute-start
  11.3 4.0 gather_fusion.8
  16.1 2.6 gather_fusion.10
  19.5 1.5 collective-permute-start.2
  21.0 4.0 gather_fusion.14
  31.0 20.9 %gather_fusion.1 = f32[6144,3]{1,0:T(8,128)} fusion(f32[3,2048]{0,1:T(8,128)S(1)} %copy.112, s32[6144]{0:T(1024)S(1)} %broadcast_clamp_fusion), kind=kCustom, calls=%fused_computation.1 | custom fusion | bytes 172032 | tf_op jit(solution)/shard_map/gather | solution.py:130
  51.9 22.1 %gather_fusion.2 = bf16[6144,64]{1,0:T(8,128)(2,1)} fusion(bf16[64,2048]{0,1:T(8,128)(2,1)S(1)} %copy.114, s32[6144]{0:T(1024)S(1)} %broadcast_clamp_fusion), kind=kCustom, calls=%fused_computation.2 | custom fusion | bytes 1597440 | tf_op jit(solution)/shard_map/gather | solution.py:131
  74.0 20.9 %gather_fusion = f32[6144,3]{1,0:T(8,128)} fusion(f32[3,2048]{0,1:T(8,128)S(1)} %copy.112, s32[6144]{0:T(1024)S(1)} %broadcast_clamp_fusion.1), kind=kCustom, calls=%fused_computation | custom fusion | bytes 172032 | tf_op jit(solution)/shard_map/gather | solution.py:132
  94.9 22.0 %gather_fusion.3 = bf16[6144,64]{1,0:T(8,128)(2,1)} fusion(bf16[64,2048]{0,1:T(8,128)(2,1)S(1)} %copy.114, s32[6144]{0:T(1024)S(1)} %broadcast_clamp_fusion.1), kind=kCustom, calls=%fused_computation.3 | custom fusion | bytes 1597440 | tf_op jit(solution)/shard_map/gather | solution.py:133
  117.6 7.6 gather_fusion.6
  125.2 6.2 gather_fusion.7
  132.0 7.6 gather_fusion.12
  139.6 8.0 %gather_fusion.13 = bf16[2048,64]{1,0:T(8,128)(2,1)} fusion(bf16[64,2048]{0,1:T(8,128)(2,1)S(1)} %copy.114, s32[2048]{0:T(1024)S(1)} %broadcast_clamp_fusion.4), kind=kCustom, calls=%fused_computation.13 | custom fusion | bytes 532480 | tf_op jit(solution)/shard_map/gather | solution.py:170
  147.6 3.0 copy.116
  150.6 3.1 copy.117
  155.1 2.5 copy.119
  158.2 1.6 copy.145
  160.3 7.6 gather_fusion.5
  167.9 1.6 copy.130
  169.8 7.6 gather_fusion.11
  177.4 1.6 copy.144
  179.0 6.2 gather_fusion.9
  185.6 17.9 %while.57 = (s32[]{:T(128)}, f32[]{:T(128)}, f32[3,2048]{1,0:T(4,128)S(1)}, f32[64,2048]{1,0:T(8,128)S(1)}, f32[3,2048]{1,0:T(4,128)S(1)}, /*index=5*/f32[64,204...) while((s32[]{:T(128)}, f32[]{:T(128)}, ...), condition=%wide.region_11.12_spmd.clone, body=%wide.region_6.11_spmd.sunk.clone.sunk | while | flops 246594080 | bytes 9612223 | solution.py:89
  187.5 2.0 convolution_bitcast_fusion.14
  189.5 1.6 fusion.370
  196.4 2.0 convolution_bitcast_fusion.14
  198.4 1.6 fusion.370
  203.5 6.2 gather_fusion.15
  210.1 20.8 %while.58 = (s32[]{:T(128)}, f32[]{:T(128)}, f32[3,2048]{1,0:T(4,128)S(1)}, f32[64,2048]{1,0:T(8,128)S(1)}, f32[3,2048]{1,0:T(4,128)S(1)}, /*index=5*/f32[64,204...) while((s32[]{:T(128)}, f32[]{:T(128)}, ...), condition=%wide.region_17.18_spmd.clone, body=%wide.region_12.17_spmd.sunk.clone.sunk | while | flops 246594080 | bytes 9743323 | solution.py:89
  213.5 2.0 convolution_bitcast_fusion.16
  215.5 1.6 fusion.400
  223.8 2.0 convolution_bitcast_fusion.16
  225.8 1.6 fusion.400
  232.2 12.0 %scatter_custom_fusion.12 = f32[64,1536]{0,1:T(8,128)S(1)} fusion(s32[2048]{0:T(1024)} %bitcast.415, f32[2048,64]{1,0:T(8,128)} %copy.162, f32[]{:T(128)} %constant.142.clone.1), kind=kCustom, calls=%fused_computation.275 | custom fusion | flops 131072 | bytes 393728 | tf_op jit(solution)/shard_map/scatter-add | solution.py:186
  245.3 10.9 %collective-permute-start.6 = (f32[64,1536]{1,0:T(8,128)}, f32[64,1536]{1,0:T(8,128)}, u32[]{:S(2)}, u32[]{:S(2)}) collective-permute-start(f32[64,1536]{1,0:T(8,128)} %copy.163), channel_id=1, source_target_pairs={{0,2},{2,4},{4,6},{6,8},{8,10},{10,12},{12,14},{14,16},{16,18},{18... | collective-permute-start | bytes 1179656 | tf_op jit(solution)/shard_map/ppermute | solution.py:14
  256.5 11.8 %scatter_custom_fusion.14 = f32[64,1536]{0,1:T(8,128)S(1)} fusion(s32[2048]{0:T(1024)} %bitcast.412, f32[2048,64]{1,0:T(8,128)S(1)} %copy.165, f32[]{:T(128)} %constant.142.clone.1), kind=kCustom, calls=%fused_computation.273 | custom fusion | flops 131072 | bytes 393728 | tf_op jit(solution)/shard_map/scatter-add | solution.py:189
  269.7 11.8 %scatter_custom_fusion.4 = f32[3,1536]{0,1:T(8,128)S(1)} fusion(s32[2048]{0:T(1024)} %bitcast.416, f32[2048,3]{1,0:T(8,128)S(1)} %copy.152, f32[]{:T(128)} %constant.142.clone.1), kind=kCustom, calls=%fused_computation.279 | custom fusion | flops 6144 | bytes 18944 | tf_op jit(solution)/shard_map/scatter-add | solution.py:185
  282.4 26.4 %collective-permute-start.4 = (f32[3,1536]{1,0:T(4,128)}, f32[3,1536]{1,0:T(4,128)}, u32[]{:S(2)}, u32[]{:S(2)}) collective-permute-start(f32[3,1536]{1,0:T(4,128)} %copy.153), channel_id=1, source_target_pairs={{0,2},{2,4},{4,6},{6,8},{8,10},{10,12},{12,14},{14,16},{16,18},{18... | collective-permute-start | bytes 55304 | tf_op jit(solution)/shard_map/ppermute | solution.py:14
  309.1 11.8 %scatter_custom_fusion.6 = f32[3,1536]{0,1:T(8,128)S(1)} fusion(s32[2048]{0:T(1024)} %bitcast.413, f32[2048,3]{1,0:T(8,128)S(1)} %copy.155, f32[]{:T(128)} %constant.142.clone.1), kind=kCustom, calls=%fused_computation.277 | custom fusion | flops 6144 | bytes 18944 | tf_op jit(solution)/shard_map/scatter-add | solution.py:188
  323.5 40.1 %while.56 = (s32[]{:T(128)}, f32[]{:T(128)}, f32[3,6144]{1,0:T(4,128)S(1)}, f32[64,6144]{1,0:T(8,128)S(1)}, f32[3,6144]{1,0:T(4,128)S(1)}, /*index=5*/f32[64,614...) while((s32[]{:T(128)}, f32[]{:T(128)}, ...), condition=%wide.region_5.6_spmd, body=%wide.region_0.5_spmd.sunk | while | flops 246594080 | bytes 9610155 | solution.py:89
  331.1 1.4 fusion.340
  344.4 1.4 fusion.340
  357.7 1.4 fusion.340
  363.6 2.3 copy.158
  365.9 2.2 copy.159
  368.1 2.2 copy.148
  370.3 2.2 copy.149
  372.5 33.7 %scatter_custom_fusion.8 = f32[64,2048]{0,1:T(8,128)S(1)} fusion(s32[6144]{0:T(1024)} %bitcast.403, f32[6144,64]{1,0:T(8,128)} %copy.158, f32[]{:T(128)} %constant.142.clone.1), kind=kCustom, calls=%fused_computation.269 | custom fusion | flops 393216 | bytes 524800 | tf_op jit(solution)/shard_map/scatter-add | solution.py:147
  406.3 33.9 %scatter_fusion.5 = f32[64,2048]{0,1:T(8,128)S(1)} fusion(f32[64,2048]{0,1:T(8,128)S(1)} %scatter_custom_fusion.8, s32[6144]{0:T(1024)S(1)} %bitcast.387, f32[6144,64]{1,0:T(8,128)} %copy.159), kind=kCustom, calls=%fused_computation.25 | custom fusion | flops 393216 | bytes 4743168 | tf_op jit(solution)/shard_map/scatter-add | solution.py:149
  440.2 33.7 %scatter_custom_fusion = f32[3,2048]{0,1:T(8,128)S(1)} fusion(s32[6144]{0:T(1024)} %bitcast.404, f32[6144,3]{1,0:T(8,128)} %copy.148, f32[]{:T(128)} %constant.142.clone.1), kind=kCustom, calls=%fused_computation.271 | custom fusion | flops 18432 | bytes 25088 | tf_op jit(solution)/shard_map/scatter-add | solution.py:142
  473.9 45.1 %psum.14 = f32[]{:T(128)} all-reduce(f32[]{:T(128)S(6)} %add.373), channel_id=1, replica_groups=mesh['gx'=16,'gy'=2] {'gy'}, use_global_device_ids=true, to_apply=%region_18.19 | all-reduce | flops 1 | bytes 8 | tf_op jit(solution)/shard_map/psum | solution.py:193
  519.0 33.9 %scatter_fusion = f32[3,2048]{0,1:T(8,128)S(1)} fusion(f32[3,2048]{0,1:T(8,128)S(1)} %scatter_custom_fusion, s32[6144]{0:T(1024)S(1)} %bitcast.388, f32[6144,3]{1,0:T(8,128)} %copy.149), kind=kCustom, calls=%fused_computation.17 | custom fusion | flops 18432 | bytes 245760 | tf_op jit(solution)/shard_map/scatter-add | solution.py:142
  552.9 105.2 %psum.15 = f32[]{:T(128)} all-reduce(f32[]{:T(128)} %psum.14), channel_id=1, replica_groups=mesh['gx'=16,'gy'=2] {'gx'}, use_global_device_ids=true, to_apply=%region_19.20 | all-reduce | flops 1 | bytes 8 | tf_op jit(solution)/shard_map/psum | solution.py:193
  659.5 2.4 copy.161
  664.6 12.3 %scatter_fusion.6 = f32[64,2048]{0,1:T(8,128)S(1)} fusion(f32[64,2048]{0,1:T(8,128)S(1)} %scatter_fusion.5, s32[2048]{0:T(1024)S(1)} %bitcast.393, f32[2048,64]{1,0:T(8,128)S(1)} %copy.160), kind=kCustom, calls=%fused_computation.26 | custom fusion | flops 131072 | bytes 1581056 | tf_op jit(solution)/shard_map/scatter-add | solution.py:167
  676.9 12.2 %scatter_fusion.7 = f32[64,2048]{0,1:T(8,128)S(1)} fusion(f32[64,2048]{0,1:T(8,128)S(1)} %scatter_fusion.6, s32[2048]{0:T(1024)S(1)} %bitcast.396, f32[2048,64]{1,0:T(8,128)} %copy.161), kind=kCustom, calls=%fused_computation.27 | custom fusion | flops 131072 | bytes 1581056 | tf_op jit(solution)/shard_map/scatter-add | solution.py:184
  689.1 12.2 %scatter_fusion.1 = f32[3,2048]{0,1:T(8,128)S(1)} fusion(f32[3,2048]{0,1:T(8,128)S(1)} %scatter_fusion, s32[2048]{0:T(1024)S(1)} %bitcast.394, f32[2048,3]{1,0:T(8,128)} %copy.150), kind=kCustom, calls=%fused_computation.18 | custom fusion | flops 6144 | bytes 81920 | tf_op jit(solution)/shard_map/scatter-add | solution.py:166
  701.4 12.2 %scatter_fusion.2 = f32[3,2048]{0,1:T(8,128)S(1)} fusion(f32[3,2048]{0,1:T(8,128)S(1)} %scatter_fusion.1, s32[2048]{0:T(1024)S(1)} %bitcast.397, f32[2048,3]{1,0:T(8,128)} %copy.151), kind=kCustom, calls=%fused_computation.19 | custom fusion | flops 6144 | bytes 81920 | tf_op jit(solution)/shard_map/scatter-add | solution.py:183
  715.3 1.9 copy.157
  717.2 9.1 %scatter_fusion.3 = f32[3,2048]{0,1:T(8,128)S(1)} fusion(f32[3,2048]{0,1:T(8,128)S(1)} %scatter_fusion.2, s32[1536]{0:T(1024)S(1)} %get-tuple-element.733, f32[1536,3]{1,0:T(8,128)S(1)} %copy.154), kind=kCustom, calls=%fused_computation.21 | custom fusion | flops 4608 | bytes 61440 | tf_op jit(solution)/shard_map/scatter-add | solution.py:191
  726.4 9.5 %scatter_fusion.4 = f32[3,2048]{0,1:T(8,128)S(1)} fusion(f32[3,2048]{0,1:T(8,128)S(1)} %scatter_fusion.3, s32[1536]{0:T(1024)S(1)} %get-tuple-element.732, f32[1536,3]{1,0:T(8,128)} %copy.157), kind=kCustom, calls=%fused_computation.23 | custom fusion | flops 4608 | bytes 61440 | tf_op jit(solution)/shard_map/scatter-add | solution.py:191
  739.5 9.3 %scatter_fusion.8 = f32[64,2048]{0,1:T(8,128)S(1)} fusion(f32[64,2048]{0,1:T(8,128)S(1)} %scatter_fusion.7, s32[1536]{0:T(1024)S(1)} %get-tuple-element.733, f32[1536,64]{1,0:T(8,128)S(1)} %copy.164), kind=kCustom, calls=%fused_computation.29 | custom fusion | flops 98304 | bytes 1185792 | tf_op jit(solution)/shard_map/scatter-add | solution.py:192
  748.8 9.1 %scatter_fusion.9 = f32[64,2048]{0,1:T(8,128)S(1)} fusion(f32[64,2048]{0,1:T(8,128)S(1)} %scatter_fusion.8, s32[1536]{0:T(1024)S(1)} %get-tuple-element.732, f32[1536,64]{1,0:T(8,128)S(1)} %copy.167), kind=kCustom, calls=%fused_computation.31 | custom fusion | flops 98304 | bytes 1185792 | tf_op jit(solution)/shard_map/scatter-add | solution.py:192
  (255 shorter events, 85.4 us)
Async XLA Ops:
  0.6 10.4 %copy-start.11 = (bf16[64,2048]{1,0:T(8,128)(2,1)S(1)}, bf16[64,2048]{1,0:T(8,128)(2,1)}, u32[]{:S(2)}) copy-start(bf16[64,2048]{1,0:T(8,128)(2,1)} %param.24) | copy-start | bytes 786436
  5.5 154.5 %collective-permute-start = (f32[3,1536]{1,0:T(4,128)S(1)}, f32[3,1536]{1,0:T(4,128)S(1)}, u32[]{:S(2)}, u32[]{:S(2)}) collective-permute-start(f32[3,1536]{1,0:T(4,128)S(1)} %copy.121), channel_id=1, source_target_pairs={{0,30},{2,0},{4,2},{6,4},{8,6},{10,8},{12,10},{14,12},{16,14},{18,... | collective-permute-start | bytes 55304 | tf_op jit(solution)/shard_map/ppermute | solution.py:14
  15.3 10.2 %copy-start.19 = (s32[4,6144]{1,0:T(4,128)S(1)}, s32[4,6144]{1,0:T(4,128)}, u32[]{:S(2)}) copy-start(s32[4,6144]{1,0:T(4,128)} %param.26) | copy-start | bytes 294916
  15.3 11.0 %copy-start.21 = (s32[4,2048]{1,0:T(4,128)S(1)}, s32[4,2048]{1,0:T(4,128)}, u32[]{:S(2)}) copy-start(s32[4,2048]{1,0:T(4,128)} %param.27) | copy-start | bytes 98308
  15.3 11.0 %copy-start.22 = (s32[4,2048]{1,0:T(4,128)S(1)}, s32[4,2048]{1,0:T(4,128)}, u32[]{:S(2)}) copy-start(s32[4,2048]{1,0:T(4,128)} %param.28) | copy-start | bytes 98308
  15.3 163.6 %collective-permute-start.1 = (bf16[64,1536]{0,1:T(8,128)(2,1)}, bf16[64,1536]{0,1:T(8,128)(2,1)S(1)}, u32[]{:S(2)}, u32[]{:S(2)}) collective-permute-start(bf16[64,1536]{0,1:T(8,128)(2,1)} %bitcast.32), channel_id=1, source_target_pairs={{0,30},{2,0},{4,2},{6,4},{8,6},{10,8},{12,10},{14,12},{16,14},{18,... | collective-permute-start | bytes 589832 | tf_op jit(solution)/shard_map/ppermute | solution.py:14
  16.1 11.0 %copy-start.26 = (s32[1,3]{1,0:T(1,128)S(1)}, s32[1,3]{1,0:T(1,128)}, u32[]{:S(2)}) copy-start(s32[1,3]{1,0:T(1,128)} %param.29) | copy-start | bytes 40
  19.5 149.9 %collective-permute-start.2 = (f32[3,1536]{1,0:T(4,128)}, f32[3,1536]{1,0:T(4,128)S(1)}, u32[]{:S(2)}, u32[]{:S(2)}) collective-permute-start(f32[3,1536]{1,0:T(4,128)} %copy.135), channel_id=1, source_target_pairs={{0,1},{1,0},{2,3},{3,2},{4,5},{5,4},{6,7},{7,6},{8,9},{9,8},{10,11... | collective-permute-start | bytes 55304 | tf_op jit(solution)/shard_map/ppermute | solution.py:14
  25.0 178.5 %collective-permute-start.3 = (bf16[64,1536]{0,1:T(8,128)(2,1)}, bf16[64,1536]{0,1:T(8,128)(2,1)S(1)}, u32[]{:S(2)}, u32[]{:S(2)}) collective-permute-start(bf16[64,1536]{0,1:T(8,128)(2,1)} %bitcast.46), channel_id=1, source_target_pairs={{0,1},{1,0},{2,3},{3,2},{4,5},{5,4},{6,7},{7,6},{8,9},{9,8},{10,11... | collective-permute-start | bytes 589832 | tf_op jit(solution)/shard_map/ppermute | solution.py:14
  25.6 48.4 %copy-start.20 = (s32[6144,1]{0,1:T(1,128)}, s32[6144,1]{0,1:T(1,128)S(1)}, u32[]{:S(2)}) copy-start(s32[6144,1]{0,1:T(1,128)S(1)} %get-tuple-element.893) | copy-start | bytes 73732
  26.3 47.7 %copy-start.24 = (s32[2048,1]{0,1:T(1,128)}, s32[2048,1]{0,1:T(1,128)S(1)}, u32[]{:S(2)}) copy-start(s32[2048,1]{0,1:T(1,128)S(1)} %get-tuple-element.902) | copy-start | bytes 24580
  26.4 2.6 copy-start.23
  150.6 3.1 copy-start.3
  155.1 2.5 copy-start.7
  157.6 2.1 copy-start.6
  178.9 6.6 copy-start
  178.9 6.6 copy-start.1
  178.9 6.6 copy-start.8
  178.9 6.6 copy-start.9
  178.9 6.6 copy-start.10
  178.9 6.6 copy-start.18
  179.0 6.6 copy-start.25
  179.0 6.6 copy-start.27
  203.5 6.2 copy-start.12
  203.5 6.4 copy-start.4
  213.2 2.3 copy-start.28
  223.5 2.3 copy-start.28
  230.8 14.4 %copy-start.5 = (f32[64,2048]{1,0:T(8,128)}, f32[64,2048]{1,0:T(8,128)S(1)}, u32[]{:S(2)}) copy-start(f32[64,2048]{1,0:T(8,128)S(1)} %get-tuple-element.376) | copy-start | bytes 1572868
  230.8 14.4 %copy-start.14 = (f32[3,2048]{1,0:T(4,128)}, f32[3,2048]{1,0:T(4,128)S(1)}, u32[]{:S(2)}) copy-start(f32[3,2048]{1,0:T(4,128)S(1)} %get-tuple-element.370) | copy-start | bytes 73732
  230.9 14.4 %copy-start.16 = (f32[3,2048]{1,0:T(4,128)}, f32[3,2048]{1,0:T(4,128)S(1)}, u32[]{:S(2)}) copy-start(f32[3,2048]{1,0:T(4,128)S(1)} %get-tuple-element.372) | copy-start | bytes 73732
  245.3 491.7 %collective-permute-start.6 = (f32[64,1536]{1,0:T(8,128)}, f32[64,1536]{1,0:T(8,128)}, u32[]{:S(2)}, u32[]{:S(2)}) collective-permute-start(f32[64,1536]{1,0:T(8,128)} %copy.163), channel_id=1, source_target_pairs={{0,2},{2,4},{4,6},{6,8},{8,10},{10,12},{12,14},{14,16},{16,18},{18... | collective-permute-start | bytes 1179656 | tf_op jit(solution)/shard_map/ppermute | solution.py:14
  256.2 13.1 %copy-start.13 = (f32[3,2048]{1,0:T(4,128)S(1)}, f32[3,2048]{1,0:T(4,128)}, u32[]{:S(2)}) copy-start(f32[3,2048]{1,0:T(4,128)} %copy-done.12) | copy-start | bytes 73732
  269.3 39.4 %copy-start.17 = (f32[3,2048]{1,0:T(4,128)S(1)}, f32[3,2048]{1,0:T(4,128)}, u32[]{:S(2)}) copy-start(f32[3,2048]{1,0:T(4,128)} %copy-done.16) | copy-start | bytes 73732
  269.3 468.9 %collective-permute-start.7 = (f32[64,1536]{1,0:T(8,128)}, f32[64,1536]{1,0:T(8,128)}, u32[]{:S(2)}, u32[]{:S(2)}) collective-permute-start(f32[64,1536]{1,0:T(8,128)} %copy.166), channel_id=1, source_target_pairs={{0,1},{1,0},{2,3},{3,2},{4,5},{5,4},{6,7},{7,6},{8,9},{9,8},{10,11... | collective-permute-start | bytes 1179656 | tf_op jit(solution)/shard_map/ppermute | solution.py:14
  282.4 431.9 %collective-permute-start.4 = (f32[3,1536]{1,0:T(4,128)}, f32[3,1536]{1,0:T(4,128)}, u32[]{:S(2)}, u32[]{:S(2)}) collective-permute-start(f32[3,1536]{1,0:T(4,128)} %copy.153), channel_id=1, source_target_pairs={{0,2},{2,4},{4,6},{6,8},{8,10},{10,12},{12,14},{14,16},{16,18},{18... | collective-permute-start | bytes 55304 | tf_op jit(solution)/shard_map/ppermute | solution.py:14
  321.7 393.6 %collective-permute-start.5 = (f32[3,1536]{1,0:T(4,128)}, f32[3,1536]{1,0:T(4,128)}, u32[]{:S(2)}, u32[]{:S(2)}) collective-permute-start(f32[3,1536]{1,0:T(4,128)} %copy.156), channel_id=1, source_target_pairs={{0,1},{1,0},{2,3},{3,2},{4,5},{5,4},{6,7},{7,6},{8,9},{9,8},{10,11... | collective-permute-start | bytes 55304 | tf_op jit(solution)/shard_map/ppermute | solution.py:14
  322.0 1.4 copy-start.29
  363.6 2.3 copy-start.2
  659.5 3.8 copy-start.15
